TPU v7x, 1024 devices: a whole 4x4x32 slice. The times are simulated.
1024 devices in a mesh: rep: 32 (over x, y, z_hi), grp: 32 (over z_lo, core).
Axes of the slice: x: 4, y: 4, z: 32 (z_hi: 2, z_lo: 16; z = z_hi * 16 + z_lo), core: 2. Of those that a mesh axis runs over, the one named last changes fastest.
Arguments:
- activations: bfloat16 [524288, 512], P(('rep', 'grp')), may hold values from -6 to 6
- out_grads: bfloat16 [524288, 1024], P(('rep', 'grp')), may hold values from -0.0014648438 to 0.0014648438
- stats_old: float32 [4, 512, 512], P(None, 'grp'), as said below
Outputs:
- stats_new: float32 [4, 512, 512], P(None, 'grp')
- update: float32 [2, 512, 512], P(None, 'grp')
Inputs may be any that keep to these rules, and one draw needn't show every extreme that they name: Each stats_old[c] is symmetric positive definite.
All inputs are finite; a program needn't handle non-finite values.
Results may differ from a plain program's by a relative error of at most 0.0009.
The roundings to bfloat16 on the way count: a program that leaves them out, or rounds other values in their place, can miss the bound.
Values may be sent and summed in bfloat16 or wider, within the bound.
A program may use at most 32 MiB of HBM per device.

v0:
```python
import math

import jax
import jax.numpy as jnp
from jax import lax
from jax.sharding import PartitionSpec as P

ITERS = 2


DAMPING = 0.01


def chain_product(start, wholes):
    running = jnp.einsum("crb,cbd->crd", start, wholes[1], preferred_element_type=jnp.float32)
    return running


def on_device(activations, out_grads, stats_old):
    block_order = activations.shape[1]
    token_count = activations.shape[0]
    tile_count = out_grads.shape[1] // block_order
    rows_dev = stats_old.shape[1]
    row_start = lax.axis_index("grp") * rows_dev
    grads_three = out_grads.reshape(token_count, tile_count, block_order)
    term_rows = jnp.einsum(
        "ktc,ki->cti", grads_three, activations, preferred_element_type=jnp.float32
    )
    partial_rows = lax.psum_scatter(
        term_rows.reshape(rows_dev * lax.axis_size("grp"), tile_count * block_order),
        "grp",
        scatter_dimension=0,
        tiled=True,
    )
    summed = lax.psum(partial_rows, "rep")
    grad_full = lax.all_gather(summed.astype(jnp.bfloat16), "grp", axis=0, tiled=True)
    grad_three = grad_full.reshape(block_order, tile_count, block_order)
    left_cols = lax.dynamic_slice_in_dim(grad_three, row_start, rows_dev, 2)
    left_rows = jnp.einsum(
        "jtr,jti->tri", left_cols, grad_three, preferred_element_type=jnp.float32
    )
    right_part = lax.dynamic_slice_in_dim(grad_three, row_start, rows_dev, 0)
    right_rows = jnp.einsum(
        "rti,jti->trj", right_part, grad_three, preferred_element_type=jnp.float32
    )
    stats_new = stats_old + jnp.concatenate([left_rows, right_rows], axis=0)
    column_ids = lax.broadcasted_iota(jnp.int32, (rows_dev, block_order), 1)
    row_ids = lax.broadcasted_iota(jnp.int32, (rows_dev, block_order), 0) + row_start
    eye_rows = (column_ids == row_ids).astype(jnp.float32)
    damped = stats_new + DAMPING * eye_rows
    squares = lax.psum(jnp.sum(damped * damped, axis=(1, 2)), "grp")
    scales = 2.5 / jnp.sqrt(squares)
    quarter = scales**0.25
    iterate_all = scales[:, None, None] * damped
    iterate = iterate_all
    whole_list = []
    first_rows = None
    for iteration in range(ITERS):
        factor = ((5.0 * eye_rows - iterate) * 0.25).astype(jnp.bfloat16)
        if iteration == 0:
            first_rows = factor
        newton_whole_factor = lax.all_gather(factor, "grp", axis=1, tiled=True)
        whole_list.append(newton_whole_factor)
        if iteration + 1 < ITERS:
            upcast = newton_whole_factor.astype(jnp.float32)
            for repeat in range(4):
                iterate = jnp.einsum(
                    "crb,cbd->crd", iterate, upcast, precision=lax.Precision.HIGHEST
                )
    first_rows, wholes = (first_rows, whole_list)
    left_wholes = [whole_factor[:tile_count] for whole_factor in wholes]
    right_wholes = [whole_factor[tile_count:] for whole_factor in wholes]
    left_roots = (
        quarter[:tile_count, None, None] * chain_product(left_wholes[0], left_wholes)
    ).astype(jnp.bfloat16)
    right_roots = (
        quarter[tile_count:, None, None] * chain_product(first_rows[tile_count:], right_wholes)
    ).astype(jnp.bfloat16)
    inner_rows = jnp.einsum(
        "trj,jti->tri", right_roots, grad_three, preferred_element_type=jnp.float32
    )
    update = jnp.einsum(
        "trm,tmi->tri", inner_rows, left_roots.astype(jnp.float32), precision=lax.Precision.HIGHEST
    ) * math.sqrt(block_order)
    return (stats_new, update)


def solution(mesh):
    in_specs = (P(("rep", "grp"), None), P(("rep", "grp"), None), P(None, "grp", None))
    out_specs = (P(None, "grp", None), P(None, "grp", None))
    return jax.shard_map(
        on_device, mesh=mesh, in_specs=in_specs, out_specs=out_specs, check_vma=False
    )
```

profile of v0, /device:TPU:1, one launch (start us, length us, event | category | flops | bytes accessed | tf_op | source)
XLA Modules:
  0.0 1991.5 jit_solution(5570742074853311145)
XLA Ops:
  7.2 0.0 copy-start
  7.2 0.0 reduce-scatter.4.cloned.1.call-start
  7.2 1.0 copy-done
  8.2 1.9 fusion.3
  10.2 1.8 copy.34
  12.0 0.0 reduce-scatter.4.cloned.1.call-update
  12.0 0.0 all-gather.4.cloned.1.call-start
  12.1 354.3 %reduce-scatter.4.cloned.1.call-done = f32[16,1024]{1,0:T(8,128)} async-done(((f32[512,1024]{1,0:T(8,128)}), f32[16,1024]{1,0:T(8,128)}) %reduce-scatter.4.cloned.1.call-update) | async-done | bytes 65552 | tf_op jit(solution)/shard_map/reduce_scatter | solution.py:29
  366.3 442.5 %psum.14 = bf16[16,1024]{1,0:T(8,128)(2,1)} all-reduce(f32[16,1024]{1,0:T(8,128)} %reduce-scatter.4.cloned.1.call-done), channel_id=1, replica_groups=mesh['rep'=32,'grp'=32] {'rep'}, use_global_device_ids=true, to_apply=%region_1.0 | all-reduce | flops 16384 | bytes 98304 | tf_op jit(solution)/shard_map/psum | solution.py:35
  808.9 0.0 all-gather.4.cloned.1.call-update
  808.9 0.0 all-gather.6.cloned.1.call-start
  808.9 0.1 fusion.16
  809.0 0.0 copy-start.5
  809.0 338.6 %all-gather.4.cloned.1.call-done = bf16[512,1024]{1,0:T(8,128)(2,1)} async-done(((bf16[16,1024]{1,0:T(8,128)(2,1)}), bf16[512,1024]{1,0:T(8,128)(2,1)}) %all-gather.4.cloned.1.call-update) | async-done | bytes 1048592 | tf_op jit(solution)/shard_map/all_gather | solution.py:36
  1147.7 1.5 copy.24
  1149.2 0.0 copy-start.2
  1149.2 0.4 fusion.9
  1149.6 0.4 fusion.18
  1150.0 0.0 copy-done.5
  1150.0 0.1 multiply_reduce_fusion
  1150.1 0.0 copy-start.3
  1150.1 167.4 %psum.15 = f32[4]{0:T(128)S(1)} all-reduce(f32[4]{0:T(128)S(1)} %get-tuple-element.2), channel_id=1, replica_groups=mesh['rep'=32,'grp'=32] {'grp'}, use_global_device_ids=true, to_apply=%region_3.0 | all-reduce | flops 4 | bytes 32 | tf_op jit(solution)/shard_map/psum | solution.py:51
  1317.5 0.7 multiply_convert_fusion.1
  1318.3 0.0 all-gather.6.cloned.1.call-update
  1318.3 0.0 all-gather.8.cloned.1.call-start
  1318.3 0.0 copy-done.2
  1318.4 328.0 %all-gather.6.cloned.1.call-done = bf16[4,512,512]{2,1,0:T(8,128)(2,1)} async-done(((bf16[4,16,512]{2,1,0:T(8,128)(2,1)}), bf16[4,512,512]{2,1,0:T(8,128)(2,1)}) %all-gather.6.cloned.1.call-update) | async-done | bytes 2097168 | tf_op jit(solution)/shard_map/all_gather | solution.py:62
  1646.3 0.0 copy-start.1
  1646.3 2.7 fusion.11
  1649.1 0.0 copy-done.1
  1649.1 0.9 fusion.23
  1650.0 0.0 copy-done.3
  1650.0 0.0 copy-start.4
  1650.0 0.9 fusion.24
  1650.9 1.6 fusion.1
  1652.5 0.0 all-gather.8.cloned.1.call-update
  1652.5 0.1 fusion.22
  1652.6 327.3 %all-gather.8.cloned.1.call-done = bf16[4,512,512]{2,1,0:T(8,128)(2,1)} async-done(((bf16[4,16,512]{2,1,0:T(8,128)(2,1)}), bf16[4,512,512]{2,1,0:T(8,128)(2,1)}) %all-gather.8.cloned.1.call-update) | async-done | bytes 2097168 | tf_op jit(solution)/shard_map/all_gather | solution.py:62
  1979.8 0.0 copy-start.6
  1979.8 0.0 copy-done.4
  1979.8 1.6 fusion.2
  1981.5 1.6 fusion.25
  1983.1 0.0 copy-done.6
  1983.1 0.7 multiply_convert_fusion
  1983.8 1.2 convolution_multiply_fusion.1
  (2 shorter events, 0.0 us)
Async XLA Ops:
  7.2 1.0 copy-start
  7.2 359.2 %reduce-scatter.4.cloned.1.call-start = ((), (), s32[]{:S(2)}) async-start(), calls=%async_computation.4 | async-start | bytes 2162688 | tf_op jit(solution)/shard_map/reduce_scatter | solution.py:29
  12.0 1135.6 %all-gather.4.cloned.1.call-start = ((), (), s32[]{:S(2)}) async-start(), calls=%async_computation.1 | async-start | bytes 1081344 | tf_op jit(solution)/shard_map/all_gather | solution.py:36
  808.9 837.5 %all-gather.6.cloned.1.call-start = ((), (), s32[]{:S(2)}) async-start(), calls=%async_computation.2 | async-start | bytes 2162688 | tf_op jit(solution)/shard_map/all_gather | solution.py:62
  809.0 341.0 %copy-start.5 = (f32[4,16,512]{2,1,0:T(8,128)S(1)}, f32[4,16,512]{2,1,0:T(8,128)}, u32[]{:S(2)}) copy-start(f32[4,16,512]{2,1,0:T(8,128)} %param.5) | copy-start | bytes 393220
  1149.2 169.2 %copy-start.2 = (bf16[512,1024]{0,1:T(8,128)(2,1)}, bf16[512,1024]{0,1:T(8,128)(2,1)S(1)}, u32[]{:S(2)}) copy-start(bf16[512,1024]{0,1:T(8,128)(2,1)S(1)} %copy.24) | copy-start | bytes 3145732
  1150.1 499.9 %copy-start.3 = (f32[4,16,512]{2,1,0:T(8,128)}, f32[4,16,512]{2,1,0:T(8,128)S(1)}, u32[]{:S(2)}) copy-start(f32[4,16,512]{2,1,0:T(8,128)S(1)} %get-tuple-element.3) | copy-start | bytes 393220
  1318.3 661.5 %all-gather.8.cloned.1.call-start = ((), (), s32[]{:S(2)}) async-start(), calls=%async_computation.3 | async-start | bytes 2162688 | tf_op jit(solution)/shard_map/all_gather | solution.py:62
  1646.3 2.7 copy-start.1
  1650.0 329.8 %copy-start.4 = (bf16[4,16,512]{2,1,0:T(8,128)(2,1)S(1)}, bf16[4,16,512]{2,1,0:T(8,128)(2,1)}, u32[]{:S(2)}) copy-start(bf16[4,16,512]{2,1,0:T(8,128)(2,1)} %multiply_convert_fusion.1) | copy-start | bytes 196612
  1979.8 3.2 copy-start.6
Sparse Core Ops, SparseCore 0:
  12.2 354.1 reduce-scatter.3
  809.0 338.6 all-gather.3
  1318.4 327.8 all-gather.5
  1652.6 327.1 all-gather.7
where the time goes:
time: 1990 us
  waiting for transfers between devices  1350 us (68%)
  blocking collectives  610 us (31%)
    all_gather x2, waiting for transfers between devices, on_device(): newton_whole_factor = lax.all_gather(factor, 'grp', axis=1, tiled=True)  655 us
    psum x1, blocking collectives, on_device(): summed = lax.psum(partial_rows, 'rep')  443 us
    reduce_scatter x1, waiting for transfers between devices, on_device(): lax.psum_scatter(term_rows.reshape(rows_dev * lax.axis_size('grp'), tile_...  354 us
    all_gather x1, waiting for transfers between devices, on_device(): lax.all_gather(summed.astype(jnp.bfloat16), 'grp', axis=0, tiled=True)  339 us
    psum x1, blocking collectives, on_device(): squares = lax.psum(jnp.sum(damped * damped, axis=(1, 2)), 'grp')  167 us
  transfers between devices with their start and end apart: 4, of which 4 were waited for; matrix products, arithmetic and copies ran while one was open for 0% of the time, Pallas kernels for 0%

commit v1 on v0

v1 whole, which is shorter than its diff:
```python
import functools
import math

import jax
import jax.numpy as jnp
from jax import lax
from jax.experimental import pallas as pl
from jax.experimental.pallas import tpu as pltpu
from jax.sharding import PartitionSpec as P

MESH = pl.DeviceIdType.MESH
F32 = jnp.float32
BF16 = jnp.bfloat16
DAMPING = 0.01
ITERS = 2


def div(a, b):
    return lax.div(a, jnp.int32(b))


def rem(a, b):
    return lax.rem(a, jnp.int32(b))


def dot(a, b):
    return jnp.dot(a, b, preferred_element_type=F32)


def transposed_dot(a, b):
    return lax.dot_general(a, b, (((0,), (0,)), ((), ())), preferred_element_type=F32)


def copy_to(src, dst, send, recv, device):
    return pltpu.make_async_remote_copy(
        src_ref=src, dst_ref=dst, send_sem=send, recv_sem=recv, device_id=device, device_id_type=MESH
    )


def kernel(
    act, og, old, stats, update,
    act_v, og_v, old_v, acc, got0, got1, got2, got3, shard, parts, blocks, pieces, grad, grad_t,
    column, planes, old_full, new_full, factor0, factor1, split, root, upd, upd_got,
    load_sem, core_send, core_recv, sum_send, sum_recv, part_send, part_recv, block_send, block_recv,
    piece_send, piece_recv, grad_send, grad_recv, near_sem, far_send, far_recv, col_send, col_recv,
    plane_send, plane_recv, out_sem, out_send, out_recv, know,
):
    rep, grp = lax.axis_index("rep"), lax.axis_index("grp")
    z_hi, xy = rem(rep, 2), div(rep, 2)
    y, x = rem(xy, 4), div(xy, 4)
    core, z_lo = rem(grp, 2), div(grp, 2)
    z = z_hi * 16 + z_lo
    blk, pos = div(z, 8), rem(z, 8)
    other = 1 - core

    def device(x_at, y_at, z_at, core_at):
        return {"rep": (x_at * 4 + y_at) * 2 + div(z_at, 16), "grp": rem(z_at, 16) * 2 + core_at}

    def along(k):
        return device(x, y, rem(z + (k + 32), 32), core)

    def in_block(k):
        return device(x, y, blk * 8 + rem(pos + k, 8), core)

    partner = device(x, y, z, other)
    hops = [
        device(x + 1 - 2 * rem(x, 2), y, z, core),
        device(3 - x, y, z, core),
        device(x, y + 1 - 2 * rem(y, 2), z, core),
        device(x, 3 - y, z, core),
    ]
    bits = [rem(rem(x, 2) + div(x, 2), 2), div(x, 2), rem(rem(y, 2) + div(y, 2), 2), div(y, 2)]
    twin = device(x, y, z_hi * 16 + rem(z_lo + 8, 16), core)

    own_cols = pl.ds(pl.multiple_of(core * 512, 512), 512)
    other_cols = pl.ds(pl.multiple_of(other * 512, 512), 512)
    loads = [
        pltpu.make_async_copy(act, act_v.at[0], load_sem.at[0]),
        pltpu.make_async_copy(og.at[:, own_cols], og_v.at[0], load_sem.at[1]),
        pltpu.make_async_copy(old.at[core], old_v.at[core, 0], load_sem.at[2]),
        pltpu.make_async_copy(old.at[core + 2], old_v.at[core, 1], load_sem.at[3]),
    ]
    for load in loads:
        load.start()

    barrier = pltpu.get_barrier_semaphore()
    for near in [partner, *hops, along(1), along(-1)]:
        pl.semaphore_signal(barrier, inc=1, device_id=near, device_id_type=MESH)
    pl.semaphore_wait(barrier, 7)

    def spread(k):
        for far in (along(1 << k), along(-(1 << k))):
            pl.semaphore_signal(know.at[k], inc=1, device_id=far, device_id_type=MESH)

    swaps = [
        copy_to(og.at[:, other_cols], og_v.at[1], core_send.at[0], core_recv.at[0], partner),
        copy_to(act, act_v.at[1], core_send.at[1], core_recv.at[1], partner),
        copy_to(old.at[other], old_v.at[core, 0], core_send.at[2], core_recv.at[2], partner),
        copy_to(old.at[other + 2], old_v.at[core, 1], core_send.at[3], core_recv.at[3], partner),
    ]
    for swap in swaps:
        swap.start()
    spread(0)

    def local_term(side, add):
        def body(m, carry):
            rows = pl.ds(pl.multiple_of(m * 128, 128), 128)
            term = transposed_dot(og_v[side, :, rows], act_v[side])
            for q in range(4):
                value = term[:, q * 128 : (q + 1) * 128]
                acc[q, rows, :] = acc[q, rows, :] + value if add else value
            return carry

        lax.fori_loop(0, 4, body, 0)

    for load in loads:
        load.wait()
    local_term(0, False)
    pl.semaphore_wait(know.at[0], 2)
    spread(1)
    swaps[0].wait_recv()
    swaps[1].wait_recv()
    local_term(1, True)

    got = [got0, got1, got2, got3]
    base = [jnp.int32(0)] * 4
    sums = []

    def send_sum(k, q):
        size = 256 >> k
        d = (q + k) % 4
        away = pl.multiple_of(base[q] + size * (1 - bits[d]), size)
        base[q] = base[q] + size * bits[d]
        copy = copy_to(
            acc.at[q, pl.ds(away, size)], got[k].at[q], sum_send.at[k, q], sum_recv.at[k, q], hops[d]
        )
        copy.start()
        sums.append(copy)

    def take_sum(k, q):
        size = 256 >> k
        sums[k * 4 + q].wait_recv()
        keep = pl.ds(pl.multiple_of(base[q], size), size)
        return acc[q, keep, :] + got[k][q], keep

    for q in range(4):
        send_sum(0, q)
    pl.semaphore_wait(know.at[1], 2)
    spread(2)
    swaps[2].wait_recv()
    swaps[3].wait_recv()

    slice_cols = pl.ds(pl.multiple_of((bits[2] * 2 + bits[3]) * 128, 128), 128)
    mine = old_v.at[bits[1], bits[0], :, slice_cols]
    half = div(z_lo, 8)
    stage = pltpu.make_async_copy(mine, column.at[pos, half], near_sem.at[0])
    stage.start()
    for k in range(1, 4):
        if k == 2:
            pl.semaphore_wait(know.at[2], 2)
            spread(3)
            far = copy_to(mine, column.at[pos, half], far_send.at[0], far_recv.at[0], twin)
            far.start()
        for q in range(4):
            value, keep = take_sum(k - 1, q)
            acc[q, keep, :] = value
            send_sum(k, q)
    stage.wait()
    for q in range(4):
        value, keep = take_sum(3, q)
        for h in range(2):
            shard[2 * q + h] = value[16 * h : 16 * h + 16]

    to_parts = []
    for k in range(1, 8):
        copy = copy_to(
            shard.at[rem(pos + k, 8)], parts.at[k - 1], part_send.at[k - 1], part_recv.at[k - 1], in_block(k)
        )
        copy.start()
        to_parts.append(copy)

    far.wait_recv()
    columns = []
    for k in range(1, 8):
        copy = copy_to(column.at[pos], column.at[pos], col_send.at[k - 1], col_recv.at[k - 1], in_block(k))
        copy.start()
        columns.append(copy)
    for copy in columns:
        copy.wait_recv()

    number = bits[0] + 2 * bits[1] + 4 * bits[2] + 8 * bits[3]
    slots = [div(number, 1 << r) + rem(number, 1 << r) * (1 << (4 - r)) for r in range(4)]
    stages = [
        pltpu.make_async_copy(column.at[pl.ds(2 * r, 2)], planes.at[r, slots[r]], near_sem.at[1 + r])
        for r in range(4)
    ]
    for copy in stages:
        copy.start()
    for copy in stages:
        copy.wait()
    spreads = []

    def send_plane(k):
        for r in range(4):
            size = 1 << k
            first = pl.ds(slots[r] - rem(slots[r], size), size)
            copy = copy_to(
                planes.at[r, first], planes.at[r, first], plane_send.at[k, r], plane_recv.at[k, r], hops[(r + k) % 4]
            )
            copy.start()
            spreads.append(copy)

    def take_plane(k):
        for r in range(4):
            spreads[4 * k + r].wait_recv()

    send_plane(0)
    take_plane(0)
    send_plane(1)

    total = shard[pos]
    for k in range(1, 8):
        to_parts[k - 1].wait_recv()
        total = total + parts[k - 1]
    blocks[blk] = total
    pl.semaphore_wait(know.at[3], 2)
    to_blocks = []
    for k in range(1, 4):
        copy = copy_to(
            blocks.at[blk], blocks.at[blk], block_send.at[k - 1], block_recv.at[k - 1], along(8 * k)
        )
        copy.start()
        to_blocks.append(copy)

    take_plane(1)
    send_plane(2)
    take_plane(2)
    send_plane(3)
    take_plane(3)

    for r in range(4):

        def lay(slot, carry):
            bit = [rem(div(slot, 1 << ((d - r) % 4)), 2) for d in range(4)]
            quarter = bit[2] * 2 + bit[3]
            for b in range(2):
                for a in range(2):
                    first = pl.multiple_of((a * 8 + 2 * r + b) * 32 + bit[1] * 16, 16)
                    old_full[bit[0], quarter, pl.ds(first, 16), :] = planes[r, slot, b, a]
            return carry

        lax.fori_loop(0, 16, lay, 0)

    for copy in to_blocks:
        copy.wait_recv()
    pieces[pos] = (((blocks[0] + blocks[1]) + blocks[2]) + blocks[3]).astype(BF16)
    to_pieces = []
    for k in range(1, 8):
        copy = copy_to(pieces.at[pos], pieces.at[pos], piece_send.at[k - 1], piece_recv.at[k - 1], in_block(k))
        copy.start()
        to_pieces.append(copy)
    for copy in to_pieces:
        copy.wait_recv()

    for q in range(4):
        for h in range(2):
            first = pl.multiple_of(base[q] + 16 * h, 16)
            grad[pl.ds(first, 16), q * 128 : (q + 1) * 128] = pieces[2 * q + h]
    gathers = []
    for k in range(3, -1, -1):
        size = 256 >> k
        for q in range(4):
            d = (q + k) % 4
            if k < 3:
                gathers[(2 - k) * 4 + q].wait_recv()
            rows = pl.ds(pl.multiple_of(base[q], size), size)
            part = grad.at[rows, q * 128 : (q + 1) * 128]
            copy = copy_to(part, part, grad_send.at[k, q], grad_recv.at[k, q], hops[d])
            copy.start()
            gathers.append(copy)
            base[q] = base[q] - size * bits[d]
    for copy in gathers[12:]:
        copy.wait_recv()

    def eye_of(m):
        row = lax.broadcasted_iota(jnp.int32, (128, 512), 0) + m * 128
        return (row == lax.broadcasted_iota(jnp.int32, (128, 512), 1)).astype(F32)

    def flip(m, carry):
        rows = pl.ds(pl.multiple_of(m * 128, 128), 128)
        grad_t[rows, :] = grad[:, rows].T
        return carry

    lax.fori_loop(0, 4, flip, 0)

    def gram(m, carry):
        rows = pl.ds(pl.multiple_of(m * 128, 128), 128)
        eye = eye_of(m)
        sums_now = []
        for chain in range(2):
            left, right = (grad_t, grad) if chain == 0 else (grad, grad_t)
            term = dot(left[rows, :], right[...])
            quarters = [old_full[chain, q, rows, :] for q in range(4)]
            value = jnp.concatenate(quarters, axis=1) + term
            new_full[chain, rows, :] = value
            damped = value + DAMPING * eye
            sums_now.append(carry[chain] + jnp.sum(damped * damped, axis=0, keepdims=True))
        return tuple(sums_now)

    zero = jnp.zeros((1, 512), F32)
    squares = lax.fori_loop(0, 4, gram, (zero, zero))
    own_first = pl.multiple_of(z_lo * 32 + 16 * core, 16)
    other_first = pl.multiple_of(z_lo * 32 + 16 * other, 16)
    outs, sends = [], []
    for chain in range(2):
        outs.append(
            pltpu.make_async_copy(
                new_full.at[chain, pl.ds(own_first, 16)], stats.at[2 * chain + core], out_sem.at[chain]
            )
        )
        sends.append(
            copy_to(
                new_full.at[chain, pl.ds(other_first, 16)], stats.at[2 * chain + core],
                out_send.at[chain], out_recv.at[chain], partner,
            )
        )
        outs[-1].start()
        sends[-1].start()

    scales = [2.5 / jnp.sqrt(jnp.sum(part, axis=1, keepdims=True)) for part in squares]
    quarters = [jnp.sqrt(jnp.sqrt(scale)) for scale in scales]

    def begin(m, carry):
        rows = pl.ds(pl.multiple_of(m * 128, 128), 128)
        eye = eye_of(m)
        for chain in range(2):
            iterate = scales[chain] * (new_full[chain, rows, :] + DAMPING * eye)
            factor0[chain, rows, :] = ((5.0 * eye - iterate) * 0.25).astype(BF16)
            high = iterate.astype(BF16)
            split[chain, 0, rows, :] = high
            split[chain, 1, rows, :] = (iterate - high.astype(F32)).astype(BF16)
        return carry

    lax.fori_loop(0, 4, begin, 0)

    def multiply(step, carry):
        for top in range(2):
            rows = slice(256 * top, 256 * top + 256)
            for chain in range(2):
                whole = factor0[chain]
                iterate = dot(split[chain, 0, rows, :], whole) + dot(split[chain, 1, rows, :], whole)
                high = iterate.astype(BF16)
                split[chain, 0, rows, :] = high
                split[chain, 1, rows, :] = (iterate - high.astype(F32)).astype(BF16)
        return carry

    lax.fori_loop(0, 3, multiply, 0)

    row_ids = lax.broadcasted_iota(jnp.int32, (256, 512), 0)
    column_ids = lax.broadcasted_iota(jnp.int32, (256, 512), 1)
    for top in range(2):
        rows = slice(256 * top, 256 * top + 256)
        eye = (row_ids + 256 * top == column_ids).astype(F32)
        for chain in range(2):
            whole = factor0[chain]
            iterate = dot(split[chain, 0, rows, :], whole) + dot(split[chain, 1, rows, :], whole)
            factor1[chain, rows, :] = ((5.0 * eye - iterate) * 0.25).astype(BF16)

    chip_rows = pl.ds(pl.multiple_of(z_lo * 32, 32), 32)
    right_root = (quarters[1] * dot(factor0[1, chip_rows, :], factor1[1])).astype(BF16)
    for top in range(2):
        rows = slice(256 * top, 256 * top + 256)
        root[rows, :] = (quarters[0] * dot(factor0[0, rows, :], factor1[0])).astype(BF16)
    inner = dot(right_root, grad[...])
    high = inner.astype(BF16)
    rest = inner - high.astype(F32)
    middle = rest.astype(BF16)
    low = (rest - middle.astype(F32)).astype(BF16)
    left_root = root[...]
    total = (dot(low, left_root) + dot(middle, left_root)) + dot(high, left_root)
    upd[...] = total * math.sqrt(512)
    outs.append(
        pltpu.make_async_copy(
            upd.at[pl.ds(pl.multiple_of(16 * core, 16), 16)], update.at[core], out_sem.at[2]
        )
    )
    sends.append(
        copy_to(
            upd.at[pl.ds(pl.multiple_of(16 * other, 16), 16)], update.at[core],
            out_send.at[2], out_recv.at[2], partner,
        )
    )
    outs[-1].start()
    sends[-1].start()

    for copy in outs:
        copy.wait()
    for copy in [*swaps, *sums, far, *to_parts, *columns, *spreads, *to_blocks, *to_pieces, *gathers, *sends]:
        copy.wait_send()
    for copy in sends:
        copy.wait_recv()


def on_device(activations, out_grads, stats_old):
    dma = pltpu.SemaphoreType.DMA
    vmem = pltpu.VMEM
    anywhere = pl.BlockSpec(memory_space=pl.ANY)
    return pl.pallas_call(
        kernel,
        out_shape=(
            jax.ShapeDtypeStruct((4, 16, 512), F32),
            jax.ShapeDtypeStruct((2, 16, 512), F32),
        ),
        in_specs=[anywhere] * 3,
        out_specs=(anywhere, anywhere),
        scratch_shapes=[
            vmem((2, 512, 512), BF16),
            vmem((2, 512, 512), BF16),
            vmem((2, 2, 16, 512), F32),
            vmem((4, 512, 128), F32),
            vmem((4, 256, 128), F32),
            vmem((4, 128, 128), F32),
            vmem((4, 64, 128), F32),
            vmem((4, 32, 128), F32),
            vmem((8, 16, 128), F32),
            vmem((7, 16, 128), F32),
            vmem((4, 16, 128), F32),
            vmem((8, 16, 128), BF16),
            vmem((512, 512), BF16),
            vmem((512, 512), BF16),
            vmem((8, 2, 16, 128), F32),
            vmem((4, 16, 2, 2, 16, 128), F32),
            vmem((2, 4, 512, 128), F32),
            vmem((2, 512, 512), F32),
            vmem((2, 512, 512), BF16),
            vmem((2, 512, 512), BF16),
            vmem((2, 2, 512, 512), BF16),
            vmem((512, 512), BF16),
            vmem((32, 512), F32),
            vmem((8, 128), F32),
            dma((4,)),
            dma((4,)), dma((4,)),
            dma((4, 4)), dma((4, 4)),
            dma((7,)), dma((7,)),
            dma((3,)), dma((3,)),
            dma((7,)), dma((7,)),
            dma((4, 4)), dma((4, 4)),
            dma((5,)),
            dma((1,)), dma((1,)),
            dma((7,)), dma((7,)),
            dma((4, 4)), dma((4, 4)),
            dma((3,)),
            dma((3,)), dma((3,)),
            pltpu.SemaphoreType.REGULAR((4,)),
        ],
        compiler_params=pltpu.CompilerParams(
            collective_id=0, has_side_effects=True, vmem_limit_bytes=56 * 1024 * 1024
        ),
    )(activations, out_grads, stats_old)


def solution(mesh):
    in_specs = (P(("rep", "grp"), None), P(("rep", "grp"), None), P(None, "grp", None))
    out_specs = (P(None, "grp", None), P(None, "grp", None))
    return jax.shard_map(
        on_device, mesh=mesh, in_specs=in_specs, out_specs=out_specs, check_vma=False
    )
```

time: 1990 us -> 103 us (0.05)
  waiting for transfers between devices: 1350 us -> 0 us
  blocking collectives: 610 us -> 0 us
  Pallas kernels: 0 us -> 100 us
    all_gather x3 -> x0, waiting for transfers between devices: 994 us -> none  [the longest x2 655 us: on_device(): newton_whole_factor = lax.all_gather(factor, 'grp', axis=1, tiled=True)]
    psum x2 -> x0, blocking collectives: 610 us -> none  [the longest x1 443 us: on_device(): summed = lax.psum(partial_rows, 'rep')]
    reduce_scatter x1 -> x0, waiting for transfers between devices: 354 us -> none  [on_device(): lax.psum_scatter(term_rows.reshape(rows_dev * lax.axis_size('grp'), tile_...]
    pallas_call x0 -> x1, Pallas kernels: none -> 100 us  [on_device(): pl.pallas_call(kernel, out_shape=(jax.ShapeDtypeStruct((4, 16, 512), F32)...]
  transfers between devices with their start and end apart: 4 -> 0, of which waited for: 4 -> 0; matrix products, arithmetic and copies ran while one was open for 0% -> 0% of each run, Pallas kernels for 0% -> 0%
where the time goes in v1:
time: 103 us
  Pallas kernels  100 us (97%)
  local copies, waits for them, and re-layouts  2.23 us (2%)
    pallas_call x1, Pallas kernels, on_device(): pl.pallas_call(kernel, out_shape=(jax.ShapeDtypeStruct((4, 16, 512), F32)...  100 us
    unnamed x4, local copies, waits for them, and re-layouts  2.23 us

profile of v1, /device:TPU:1, one launch (start us, length us, event | category | flops | bytes accessed | tf_op | source)
XLA Modules:
  0.0 103.3 jit_solution(5857888068426783922)
XLA Ops:
  0.6 100.4 %shard_map.50 = (f32[4,16,512]{2,1,0:T(8,128)}, f32[2,16,512]{2,1,0:T(8,128)}) custom-call(bf16[512,512]{1,0:T(8,128)(2,1)} %act.1, bf16[512,1024]{1,0:T(8,128)(2,1)} %og.1, f32[4,16,512]{2,1,0:T(8,128)} %old.1), custom_call_target="tpu_custom_call" | custom-call | tf_op jit(solution)/shard_map/pallas_call | solution.py:408
  101.0 0.0 copy-start
  101.1 1.6 %copy.7 = f32[4,16,512]{2,1,0:T(8,128)} copy(f32[4,16,512]{2,1,0:T(8,128)} %get-tuple-element.4) | data formatting | bytes 262144
  102.7 0.0 copy-done
  102.7 0.6 copy.8
Async XLA Ops:
  101.0 1.6 %copy-start = (f32[2,16,512]{2,1,0:T(8,128)S(1)}, f32[2,16,512]{2,1,0:T(8,128)}, u32[]{:S(2)}) copy-start(f32[2,16,512]{2,1,0:T(8,128)} %get-tuple-element.5) | copy-start | bytes 196612

commit v2 on v1

--- a/solution.py
+++ b/solution.py
@@ -39,10 +39,10 @@
 
 def kernel(
     act, og, old, stats, update,
-    act_v, og_v, old_v, acc, got0, got1, got2, got3, shard, parts, blocks, pieces, grad, grad_t,
-    column, planes, old_full, new_full, factor0, factor1, split, root, upd, upd_got,
+    act_v, og_v, old_v, acc, got0, got1, shard, parts, blocks, pieces, grad, grad_t,
+    column, planes, old_full, new_full, factor0, factor1, split, root, upd,
     load_sem, core_send, core_recv, sum_send, sum_recv, part_send, part_recv, block_send, block_recv,
-    piece_send, piece_recv, grad_send, grad_recv, near_sem, far_send, far_recv, col_send, col_recv,
+    piece_send, piece_recv, grad_send, grad_recv, near_sem, col_send, col_recv,
     plane_send, plane_recv, out_sem, out_send, out_recv, know,
 ):
     rep, grp = lax.axis_index("rep"), lax.axis_index("grp")
@@ -59,18 +59,20 @@
     def along(k):
         return device(x, y, rem(z + (k + 32), 32), core)
 
-    def in_block(k):
-        return device(x, y, blk * 8 + rem(pos + k, 8), core)
-
     partner = device(x, y, z, other)
-    hops = [
-        device(x + 1 - 2 * rem(x, 2), y, z, core),
-        device(3 - x, y, z, core),
-        device(x, y + 1 - 2 * rem(y, 2), z, core),
-        device(x, 3 - y, z, core),
+    x_at = [x + 1 - 2 * rem(x, 2), 3 - x]
+    y_at = [y + 1 - 2 * rem(y, 2), 3 - y]
+    bits = [rem(rem(x, 2) + div(x, 2), 2), rem(rem(y, 2) + div(y, 2), 2), div(x, 2), div(y, 2)]
+    hops = [device(x_at[0], y, z, core), device(x, y_at[0], z, core), device(x_at[1], y, z, core), device(x, y_at[1], z, core)]
+    across = [
+        device(x_at[0], y_at[0], z, core),
+        device(x_at[1], y_at[0], z, core),
+        device(x_at[1], y_at[1], z, core),
+        device(x_at[0], y_at[1], z, core),
     ]
-    bits = [rem(rem(x, 2) + div(x, 2), 2), div(x, 2), rem(rem(y, 2) + div(y, 2), 2), div(y, 2)]
-    twin = device(x, y, z_hi * 16 + rem(z_lo + 8, 16), core)
+
+    def trio(d):
+        return [(across[d], 1, 1), (hops[d], 1, 0), (hops[(d + 1) % 4], 0, 1)]
 
     own_cols = pl.ds(pl.multiple_of(core * 512, 512), 512)
     other_cols = pl.ds(pl.multiple_of(other * 512, 512), 512)
@@ -84,107 +86,111 @@
         load.start()
 
     barrier = pltpu.get_barrier_semaphore()
-    for near in [partner, *hops, along(1), along(-1)]:
+    for near in [partner, *hops, *across, along(1), along(-1)]:
         pl.semaphore_signal(barrier, inc=1, device_id=near, device_id_type=MESH)
-    pl.semaphore_wait(barrier, 7)
+    pl.semaphore_wait(barrier, 11)
 
     def spread(k):
         for far in (along(1 << k), along(-(1 << k))):
             pl.semaphore_signal(know.at[k], inc=1, device_id=far, device_id_type=MESH)
 
-    swaps = [
-        copy_to(og.at[:, other_cols], og_v.at[1], core_send.at[0], core_recv.at[0], partner),
-        copy_to(act, act_v.at[1], core_send.at[1], core_recv.at[1], partner),
-        copy_to(old.at[other], old_v.at[core, 0], core_send.at[2], core_recv.at[2], partner),
-        copy_to(old.at[other + 2], old_v.at[core, 1], core_send.at[3], core_recv.at[3], partner),
+    swaps = []
+    for t in range(2):
+        half_rows = slice(256 * t, 256 * t + 256)
+        swaps += [
+            copy_to(og.at[half_rows, other_cols], og_v.at[1, half_rows], core_send.at[2 * t], core_recv.at[2 * t], partner),
+            copy_to(act.at[half_rows], act_v.at[1, half_rows], core_send.at[2 * t + 1], core_recv.at[2 * t + 1], partner),
+        ]
+    swaps += [
+        copy_to(old.at[other], old_v.at[core, 0], core_send.at[4], core_recv.at[4], partner),
+        copy_to(old.at[other + 2], old_v.at[core, 1], core_send.at[5], core_recv.at[5], partner),
     ]
     for swap in swaps:
         swap.start()
     spread(0)
 
-    def local_term(side, add):
-        def body(m, carry):
-            rows = pl.ds(pl.multiple_of(m * 128, 128), 128)
-            term = transposed_dot(og_v[side, :, rows], act_v[side])
-            for q in range(4):
-                value = term[:, q * 128 : (q + 1) * 128]
-                acc[q, rows, :] = acc[q, rows, :] + value if add else value
-            return carry
-
-        lax.fori_loop(0, 4, body, 0)
+    def local_term(side, first, count, add):
+        for m in range(4):
+            rows = slice(128 * m, 128 * m + 128)
+            grad_t[rows, first : first + count] = og_v[side, first : first + count, rows].T
+        term = dot(grad_t[:, first : first + count], act_v[side, first : first + count])
+        for q in range(4):
+            value = term[:, q * 128 : (q + 1) * 128]
+            acc[q] = acc[q] + value if add else value
 
     for load in loads:
         load.wait()
-    local_term(0, False)
+    local_term(0, 0, 512, False)
     pl.semaphore_wait(know.at[0], 2)
     spread(1)
-    swaps[0].wait_recv()
-    swaps[1].wait_recv()
-    local_term(1, True)
-
-    got = [got0, got1, got2, got3]
+    for t in range(2):
+        swaps[2 * t].wait_recv()
+        swaps[2 * t + 1].wait_recv()
+        local_term(1, 256 * t, 256, True)
+
+    got = [got0, got1]
     base = [jnp.int32(0)] * 4
     sums = []
 
     def send_sum(k, q):
-        size = 256 >> k
-        d = (q + k) % 4
-        away = pl.multiple_of(base[q] + size * (1 - bits[d]), size)
-        base[q] = base[q] + size * bits[d]
-        copy = copy_to(
-            acc.at[q, pl.ds(away, size)], got[k].at[q], sum_send.at[k, q], sum_recv.at[k, q], hops[d]
-        )
-        copy.start()
-        sums.append(copy)
+        size = 128 >> (2 * k)
+        d = (q + 2 * k) % 4
+        first, second = bits[d], bits[(d + 1) % 4]
+        for e, (to, a, b) in enumerate(trio(d)):
+            j = (first + a - 2 * a * first) * 2 + (second + b - 2 * b * second)
+            away = pl.multiple_of(base[q] + size * j, size)
+            copy = copy_to(
+                acc.at[q, pl.ds(away, size)], got[k].at[q, e], sum_send.at[k, q, e], sum_recv.at[k, q, e], to
+            )
+            copy.start()
+            sums.append(copy)
+        base[q] = base[q] + size * (first * 2 + second)
 
     def take_sum(k, q):
-        size = 256 >> k
-        sums[k * 4 + q].wait_recv()
+        size = 128 >> (2 * k)
         keep = pl.ds(pl.multiple_of(base[q], size), size)
-        return acc[q, keep, :] + got[k][q], keep
+        for e in range(3):
+            sums[k * 12 + q * 3 + e].wait_recv()
+        return (acc[q, keep, :] + got[k][q, 0]) + (got[k][q, 1] + got[k][q, 2]), keep
 
     for q in range(4):
         send_sum(0, q)
     pl.semaphore_wait(know.at[1], 2)
     spread(2)
-    swaps[2].wait_recv()
-    swaps[3].wait_recv()
+    swaps[4].wait_recv()
+    swaps[5].wait_recv()
 
     slice_cols = pl.ds(pl.multiple_of((bits[2] * 2 + bits[3]) * 128, 128), 128)
     mine = old_v.at[bits[1], bits[0], :, slice_cols]
     half = div(z_lo, 8)
     stage = pltpu.make_async_copy(mine, column.at[pos, half], near_sem.at[0])
     stage.start()
-    for k in range(1, 4):
-        if k == 2:
-            pl.semaphore_wait(know.at[2], 2)
-            spread(3)
-            far = copy_to(mine, column.at[pos, half], far_send.at[0], far_recv.at[0], twin)
-            far.start()
-        for q in range(4):
-            value, keep = take_sum(k - 1, q)
-            acc[q, keep, :] = value
-            send_sum(k, q)
+    pl.semaphore_wait(know.at[2], 2)
+    spread(3)
+    columns = []
+    for i, k in enumerate([8, -7, 7, -6, 6, -5, 5, -4, 4, -3, 3, -2, 2, -1, 1]):
+        copy = copy_to(mine, column.at[pos, half], col_send.at[i], col_recv.at[i], along(k))
+        copy.start()
+        columns.append(copy)
+    for q in range(4):
+        value, keep = take_sum(0, q)
+        acc[q, keep, :] = value
+        send_sum(1, q)
     stage.wait()
     for q in range(4):
-        value, keep = take_sum(3, q)
+        value, keep = take_sum(1, q)
         for h in range(2):
             shard[2 * q + h] = value[16 * h : 16 * h + 16]
 
+    around = [-4, 3, -3, 2, -2, 1, -1]
     to_parts = []
-    for k in range(1, 8):
+    for i, k in enumerate(around):
         copy = copy_to(
-            shard.at[rem(pos + k, 8)], parts.at[k - 1], part_send.at[k - 1], part_recv.at[k - 1], in_block(k)
+            shard.at[rem(pos + (k + 8), 8)], parts.at[i], part_send.at[i], part_recv.at[i], along(k)
         )
         copy.start()
         to_parts.append(copy)
 
-    far.wait_recv()
-    columns = []
-    for k in range(1, 8):
-        copy = copy_to(column.at[pos], column.at[pos], col_send.at[k - 1], col_recv.at[k - 1], in_block(k))
-        copy.start()
-        columns.append(copy)
     for copy in columns:
         copy.wait_recv()
 
@@ -202,26 +208,25 @@
 
     def send_plane(k):
         for r in range(4):
-            size = 1 << k
+            size = 1 << (2 * k)
             first = pl.ds(slots[r] - rem(slots[r], size), size)
-            copy = copy_to(
-                planes.at[r, first], planes.at[r, first], plane_send.at[k, r], plane_recv.at[k, r], hops[(r + k) % 4]
-            )
-            copy.start()
-            spreads.append(copy)
+            for e, (to, _, _) in enumerate(trio((r + 2 * k) % 4)):
+                copy = copy_to(
+                    planes.at[r, first], planes.at[r, first], plane_send.at[k, r, e], plane_recv.at[k, r, e], to
+                )
+                copy.start()
+                spreads.append(copy)
 
     def take_plane(k):
-        for r in range(4):
-            spreads[4 * k + r].wait_recv()
+        for copy in spreads[12 * k : 12 * k + 12]:
+            copy.wait_recv()
 
     send_plane(0)
-    take_plane(0)
-    send_plane(1)
 
     total = shard[pos]
-    for k in range(1, 8):
-        to_parts[k - 1].wait_recv()
-        total = total + parts[k - 1]
+    for i in range(7):
+        to_parts[i].wait_recv()
+        total = total + parts[i]
     blocks[blk] = total
     pl.semaphore_wait(know.at[3], 2)
     to_blocks = []
@@ -232,12 +237,39 @@
         copy.start()
         to_blocks.append(copy)
 
+    take_plane(0)
+    send_plane(1)
+
+    for copy in to_blocks:
+        copy.wait_recv()
+    pieces[pos] = (((blocks[0] + blocks[1]) + blocks[2]) + blocks[3]).astype(BF16)
+    to_pieces = []
+    for i, k in enumerate(around):
+        copy = copy_to(pieces.at[pos], pieces.at[pos], piece_send.at[i], piece_recv.at[i], along(k))
+        copy.start()
+        to_pieces.append(copy)
+    for copy in to_pieces:
+        copy.wait_recv()
+
+    for q in range(4):
+        for h in range(2):
+            first = pl.multiple_of(base[q] + 16 * h, 16)
+            grad[pl.ds(first, 16), q * 128 : (q + 1) * 128] = pieces[2 * q + h]
+    gathers = []
+
+    def send_grad(k):
+        size = 128 >> (2 * k)
+        for q in range(4):
+            d = (q + 2 * k) % 4
+            part = grad.at[pl.ds(pl.multiple_of(base[q], size), size), q * 128 : (q + 1) * 128]
+            for e, (to, _, _) in enumerate(trio(d)):
+                copy = copy_to(part, part, grad_send.at[k, q, e], grad_recv.at[k, q, e], to)
+                copy.start()
+                gathers.append(copy)
+            base[q] = base[q] - size * (bits[d] * 2 + bits[(d + 1) % 4])
+
+    send_grad(1)
     take_plane(1)
-    send_plane(2)
-    take_plane(2)
-    send_plane(3)
-    take_plane(3)
-
     for r in range(4):
 
         def lay(slot, carry):
@@ -251,34 +283,9 @@
 
         lax.fori_loop(0, 16, lay, 0)
 
-    for copy in to_blocks:
-        copy.wait_recv()
-    pieces[pos] = (((blocks[0] + blocks[1]) + blocks[2]) + blocks[3]).astype(BF16)
-    to_pieces = []
-    for k in range(1, 8):
-        copy = copy_to(pieces.at[pos], pieces.at[pos], piece_send.at[k - 1], piece_recv.at[k - 1], in_block(k))
-        copy.start()
-        to_pieces.append(copy)
-    for copy in to_pieces:
-        copy.wait_recv()
-
-    for q in range(4):
-        for h in range(2):
-            first = pl.multiple_of(base[q] + 16 * h, 16)
-            grad[pl.ds(first, 16), q * 128 : (q + 1) * 128] = pieces[2 * q + h]
-    gathers = []
-    for k in range(3, -1, -1):
-        size = 256 >> k
-        for q in range(4):
-            d = (q + k) % 4
-            if k < 3:
-                gathers[(2 - k) * 4 + q].wait_recv()
-            rows = pl.ds(pl.multiple_of(base[q], size), size)
-            part = grad.at[rows, q * 128 : (q + 1) * 128]
-            copy = copy_to(part, part, grad_send.at[k, q], grad_recv.at[k, q], hops[d])
-            copy.start()
-            gathers.append(copy)
-            base[q] = base[q] - size * bits[d]
+    for copy in gathers:
+        copy.wait_recv()
+    send_grad(0)
     for copy in gathers[12:]:
         copy.wait_recv()
 
@@ -291,7 +298,7 @@
         grad_t[rows, :] = grad[:, rows].T
         return carry
 
-    lax.fori_loop(0, 4, flip, 0)
+    lax.fori_loop(0, 4, flip, 0, unroll=True)
 
     def gram(m, carry):
         rows = pl.ds(pl.multiple_of(m * 128, 128), 128)
@@ -308,7 +315,7 @@
         return tuple(sums_now)
 
     zero = jnp.zeros((1, 512), F32)
-    squares = lax.fori_loop(0, 4, gram, (zero, zero))
+    squares = lax.fori_loop(0, 4, gram, (zero, zero), unroll=True)
     own_first = pl.multiple_of(z_lo * 32 + 16 * core, 16)
     other_first = pl.multiple_of(z_lo * 32 + 16 * other, 16)
     outs, sends = [], []
@@ -341,17 +348,15 @@
             split[chain, 1, rows, :] = (iterate - high.astype(F32)).astype(BF16)
         return carry
 
-    lax.fori_loop(0, 4, begin, 0)
+    lax.fori_loop(0, 4, begin, 0, unroll=True)
 
     def multiply(step, carry):
-        for top in range(2):
-            rows = slice(256 * top, 256 * top + 256)
-            for chain in range(2):
-                whole = factor0[chain]
-                iterate = dot(split[chain, 0, rows, :], whole) + dot(split[chain, 1, rows, :], whole)
-                high = iterate.astype(BF16)
-                split[chain, 0, rows, :] = high
-                split[chain, 1, rows, :] = (iterate - high.astype(F32)).astype(BF16)
+        for chain in range(2):
+            whole = factor0[chain]
+            iterate = dot(split[chain, 0], whole) + dot(split[chain, 1], whole)
+            high = iterate.astype(BF16)
+            split[chain, 0] = high
+            split[chain, 1] = (iterate - high.astype(F32)).astype(BF16)
         return carry
 
     lax.fori_loop(0, 3, multiply, 0)
@@ -395,7 +400,7 @@
 
     for copy in outs:
         copy.wait()
-    for copy in [*swaps, *sums, far, *to_parts, *columns, *spreads, *to_blocks, *to_pieces, *gathers, *sends]:
+    for copy in [*swaps, *sums, *to_parts, *columns, *spreads, *to_blocks, *to_pieces, *gathers, *sends]:
         copy.wait_send()
     for copy in sends:
         copy.wait_recv()
@@ -408,20 +413,18 @@
     return pl.pallas_call(
         kernel,
         out_shape=(
-            jax.ShapeDtypeStruct((4, 16, 512), F32),
-            jax.ShapeDtypeStruct((2, 16, 512), F32),
+            pltpu.VMEM((4, 16, 512), F32),
+            pltpu.VMEM((2, 16, 512), F32),
         ),
         in_specs=[anywhere] * 3,
-        out_specs=(anywhere, anywhere),
+        out_specs=(pl.BlockSpec(memory_space=pltpu.VMEM),) * 2,
         scratch_shapes=[
             vmem((2, 512, 512), BF16),
             vmem((2, 512, 512), BF16),
             vmem((2, 2, 16, 512), F32),
             vmem((4, 512, 128), F32),
-            vmem((4, 256, 128), F32),
-            vmem((4, 128, 128), F32),
-            vmem((4, 64, 128), F32),
-            vmem((4, 32, 128), F32),
+            vmem((4, 3, 128, 128), F32),
+            vmem((4, 3, 32, 128), F32),
             vmem((8, 16, 128), F32),
             vmem((7, 16, 128), F32),
             vmem((4, 16, 128), F32),
@@ -437,18 +440,16 @@
             vmem((2, 2, 512, 512), BF16),
             vmem((512, 512), BF16),
             vmem((32, 512), F32),
-            vmem((8, 128), F32),
             dma((4,)),
-            dma((4,)), dma((4,)),
-            dma((4, 4)), dma((4, 4)),
+            dma((6,)), dma((6,)),
+            dma((2, 4, 3)), dma((2, 4, 3)),
             dma((7,)), dma((7,)),
             dma((3,)), dma((3,)),
             dma((7,)), dma((7,)),
-            dma((4, 4)), dma((4, 4)),
+            dma((2, 4, 3)), dma((2, 4, 3)),
             dma((5,)),
-            dma((1,)), dma((1,)),
-            dma((7,)), dma((7,)),
-            dma((4, 4)), dma((4, 4)),
+            dma((15,)), dma((15,)),
+            dma((2, 4, 3)), dma((2, 4, 3)),
             dma((3,)),
             dma((3,)), dma((3,)),
             pltpu.SemaphoreType.REGULAR((4,)),

time: 103 us -> 82 us (0.80)
  Pallas kernels: 100 us -> 80 us
    pallas_call x1, Pallas kernels: 100 us -> 80 us  [on_device(): pl.pallas_call(kernel, out_shape=(pltpu.VMEM((4, 16, 512), F32), pltpu.VM...]
    unnamed x4 -> x2, local copies, waits for them, and re-layouts: 2.23 us -> 1.29 us
where the time goes in v2:
time: 82 us; the launch traced here: 81.9 us
  Pallas kernels  80 us (98%)
  local copies, waits for them, and re-layouts  1.29 us (2%)
    pallas_call x1, Pallas kernels, on_device(): pl.pallas_call(kernel, out_shape=(pltpu.VMEM((4, 16, 512), F32), pltpu.VM...  80 us

profile of v2, /device:TPU:1, one launch (start us, length us, event | category | flops | bytes accessed | tf_op | source)
XLA Modules:
  0.0 81.9 jit_solution(13258562914303392135)
XLA Ops:
  0.6 80.0 %shard_map.50 = (f32[4,16,512]{2,1,0:T(8,128)S(1)}, f32[2,16,512]{2,1,0:T(8,128)S(1)}) custom-call(bf16[512,512]{1,0:T(8,128)(2,1)} %act.1, bf16[512,1024]{1,0:T(8,128)(2,1)} %og.1, f32[4,16,512]{2,1,0:T(8,128)} %old.1), custom_call_target="tpu_custom_call" | custom-call | tf_op jit(solution)/shard_map/pallas_call | solution.py:413
  80.6 0.7 copy.7
  81.3 0.6 copy.8

commit v3 on v2

v3 whole, which is shorter than its diff:
```python
import functools
import math

import jax
import jax.numpy as jnp
from jax import lax
from jax.experimental import pallas as pl
from jax.experimental.pallas import tpu as pltpu
from jax.sharding import PartitionSpec as P

MESH = pl.DeviceIdType.MESH
F32 = jnp.float32
BF16 = jnp.bfloat16
DAMPING = 0.01
ITERS = 2


SWAP, OLD, SUM, MID, PART, BLOCK, PIECE, NEAR_GRAD, GRAD, COLUMN, NEAR_PLANE, PLANE, OUT = (
    0, 2, 3, 7, 8, 9, 10, 11, 14, 15, 16, 19, 20
)


def wait_bytes(ref, sem):
    pltpu.make_async_copy(ref, ref, sem).wait()


def div(a, b):
    return lax.div(a, jnp.int32(b))


def rem(a, b):
    return lax.rem(a, jnp.int32(b))


def dot(a, b):
    return jnp.dot(a, b, preferred_element_type=F32)


def transposed_dot(a, b):
    return lax.dot_general(a, b, (((0,), (0,)), ((), ())), preferred_element_type=F32)


def copy_to(src, dst, send, recv, device):
    return pltpu.make_async_remote_copy(
        src_ref=src, dst_ref=dst, send_sem=send, recv_sem=recv, device_id=device, device_id_type=MESH
    )


def kernel(
    act, og, old, stats, update,
    act_v, og_v, old_v, acc, got0, got1, shard, parts, blocks, pieces, grad, grad_t,
    column, planes, old_full, new_full, factor0, factor1, split, root, upd,
    here, sent, come, know,
):
    rep, grp = lax.axis_index("rep"), lax.axis_index("grp")
    z_hi, xy = rem(rep, 2), div(rep, 2)
    y, x = rem(xy, 4), div(xy, 4)
    core, z_lo = rem(grp, 2), div(grp, 2)
    z = z_hi * 16 + z_lo
    blk, pos = div(z, 8), rem(z, 8)
    other = 1 - core

    def device(x_at, y_at, z_at, core_at):
        return {"rep": (x_at * 4 + y_at) * 2 + div(z_at, 16), "grp": rem(z_at, 16) * 2 + core_at}

    def along(k):
        return device(x, y, rem(z + (k + 32), 32), core)

    partner = device(x, y, z, other)
    x_at = [x + 1 - 2 * rem(x, 2), 3 - x]
    y_at = [y + 1 - 2 * rem(y, 2), 3 - y]
    bits = [rem(rem(x, 2) + div(x, 2), 2), rem(rem(y, 2) + div(y, 2), 2), div(x, 2), div(y, 2)]
    hops = [device(x_at[0], y, z, core), device(x, y_at[0], z, core), device(x_at[1], y, z, core), device(x, y_at[1], z, core)]
    across = [
        device(x_at[0], y_at[0], z, core),
        device(x_at[1], y_at[0], z, core),
        device(x_at[1], y_at[1], z, core),
        device(x_at[0], y_at[1], z, core),
    ]

    def chip_of(d, e):
        return (across[d], hops[d], hops[(d + 1) % 4])[e]

    def number_of(d, e):
        first, second = bits[d], bits[(d + 1) % 4]
        if e in (0, 1):
            first = 1 - first
        if e in (0, 2):
            second = 1 - second
        return first * 2 + second

    barrier = pltpu.get_barrier_semaphore()
    for near in [partner, *hops, *across, along(1), along(-1)]:
        pl.semaphore_signal(barrier, inc=1, device_id=near, device_id_type=MESH)

    own_cols = pl.ds(pl.multiple_of(core * 512, 512), 512)
    other_cols = pl.ds(pl.multiple_of(other * 512, 512), 512)
    loads = [
        pltpu.make_async_copy(act, act_v.at[0], here.at[0]),
        pltpu.make_async_copy(og.at[:, own_cols], og_v.at[0], here.at[0]),
        pltpu.make_async_copy(old.at[core], old_v.at[core, 0], here.at[1]),
        pltpu.make_async_copy(old.at[core + 2], old_v.at[core, 1], here.at[1]),
    ]
    for load in loads:
        load.start()

    pl.semaphore_wait(barrier, 11)

    def spread(k):
        for far in (along(1 << k), along(-(1 << k))):
            pl.semaphore_signal(know.at[k], inc=1, device_id=far, device_id_type=MESH)

    swaps = []
    for t in range(2):
        half_rows = slice(256 * t, 256 * t + 256)
        pair = sent.at[SWAP + t], come.at[SWAP + t], partner
        swaps += [
            copy_to(og.at[half_rows, other_cols], og_v.at[1, half_rows], *pair),
            copy_to(act.at[half_rows], act_v.at[1, half_rows], *pair),
        ]
    pair = sent.at[OLD], come.at[OLD], partner
    swaps += [
        copy_to(old.at[other], old_v.at[core, 0], *pair),
        copy_to(old.at[other + 2], old_v.at[core, 1], *pair),
    ]
    for swap in swaps:
        swap.start()
    spread(0)

    def local_term(side, first, count, add):
        for m in range(4):
            rows = slice(128 * m, 128 * m + 128)
            grad_t[rows, first : first + count] = og_v[side, first : first + count, rows].T
        term = dot(grad_t[:, first : first + count], act_v[side, first : first + count])
        for q in range(4):
            value = term[:, q * 128 : (q + 1) * 128]
            acc[q] = acc[q] + value if add else value

    wait_bytes(og_v, here.at[0])
    local_term(0, 0, 512, False)
    for t in range(2):
        wait_bytes(og_v.at[1], come.at[SWAP + t])
        local_term(1, 256 * t, 256, True)

    def rows_at(q, e, s):
        return pl.ds(pl.multiple_of(128 * number_of(q, e) + 32 * number_of((q + 2) % 4, s), 32), 32)

    sums = {}
    for s in range(4):
        for q in range(4):
            for e in range(3):
                sums[q, e, s] = copy_to(
                    acc.at[q, rows_at(q, e, s)], got0.at[s, q, e], sent.at[SUM + s], come.at[SUM + s], chip_of(q, e)
                )
                sums[q, e, s].start()
    pl.semaphore_wait(know.at[0], 2)
    spread(1)
    wait_bytes(old_v.at[0], here.at[1])
    wait_bytes(old_v.at[0], come.at[OLD])

    slice_cols = pl.ds(pl.multiple_of((bits[2] * 2 + bits[3]) * 128, 128), 128)
    mine = old_v.at[bits[1], bits[0], :, slice_cols]
    half = div(z_lo, 8)
    stage = pltpu.make_async_copy(mine, column.at[pos, half], here.at[2])
    stage.start()
    pl.semaphore_wait(know.at[1], 2)
    spread(2)

    def take_sum(q, s):
        return (acc[q, rows_at(q, 3, s), :] + got0[s, q, 0]) + (got0[s, q, 1] + got0[s, q, 2])

    mids = {}
    columns = []
    for s in range(3):
        wait_bytes(got0.at[s], come.at[SUM + s])
        for q in range(4):
            acc[q, rows_at(q, 3, s), :] = take_sum(q, s)
            mids[q, s] = copy_to(
                acc.at[q, rows_at(q, 3, s)], got1.at[q, s], sent.at[MID], come.at[MID], chip_of((q + 2) % 4, s)
            )
            mids[q, s].start()
        if s == 0:
            stage.wait()
            pl.semaphore_wait(know.at[2], 2)
            spread(3)
            for i, k in enumerate([8, -7, 7, -6, 6, -5, 5, -4, 4, -3, 3, -2, 2, -1, 1]):
                copy = copy_to(mine, column.at[pos, half], sent.at[COLUMN], come.at[COLUMN], along(k))
                copy.start()
                columns.append(copy)
    wait_bytes(got0.at[3], come.at[SUM + 3])
    wait_bytes(got1, come.at[MID])
    for q in range(4):
        value = take_sum(q, 3)
        value = value + ((got1[q, 0] + got1[q, 1]) + got1[q, 2])
        for h in range(2):
            shard[2 * q + h] = value[16 * h : 16 * h + 16]

    around = [-4, 3, -3, 2, -2, 1, -1]
    to_parts = []
    for i, k in enumerate(around):
        copy = copy_to(
            shard.at[rem(pos + (k + 8), 8)], parts.at[i], sent.at[PART], come.at[PART], along(k)
        )
        copy.start()
        to_parts.append(copy)

    wait_bytes(old_full.at[0, 0, pl.ds(0, 240)], come.at[COLUMN])

    number = bits[0] + 2 * bits[1] + 4 * bits[2] + 8 * bits[3]
    slots = [div(number, 1 << r) + rem(number, 1 << r) * (1 << (4 - r)) for r in range(4)]
    stages = [
        pltpu.make_async_copy(column.at[pl.ds(2 * r, 2)], planes.at[r, slots[r]], here.at[3])
        for r in range(4)
    ]
    for copy in stages:
        copy.start()
    wait_bytes(planes.at[0, pl.ds(0, 4)], here.at[3])
    near_planes, far_planes = {}, {}

    def slots_at(r, e):
        flip = number_of(r, e)
        first, second = div(flip, 2), rem(flip, 2)
        return slots[r] - rem(slots[r], 4) + first + 2 * second

    def forward_plane(s):
        if s < 3:
            wait_bytes(planes.at[0, pl.ds(0, 4)], come.at[NEAR_PLANE + s])
        for r in range(4):
            at = slots_at(r, s)
            for e in range(3):
                far_planes[r, e, s] = copy_to(
                    planes.at[r, at], planes.at[r, at], sent.at[PLANE], come.at[PLANE], chip_of((r + 2) % 4, e)
                )
                far_planes[r, e, s].start()

    for r in range(4):
        for e in range(3):
            near_planes[r, e] = copy_to(
                planes.at[r, slots[r]], planes.at[r, slots[r]], sent.at[NEAR_PLANE + e], come.at[NEAR_PLANE + e], chip_of(r, e)
            )
            near_planes[r, e].start()
    forward_plane(3)

    total = shard[pos]
    for i in range(7):
        if i == 0:
            wait_bytes(parts, come.at[PART])
        total = total + parts[i]
    blocks[blk] = total
    pl.semaphore_wait(know.at[3], 2)
    to_blocks = []
    for k in range(1, 4):
        copy = copy_to(
            blocks.at[blk], blocks.at[blk], sent.at[BLOCK], come.at[BLOCK], along(8 * k)
        )
        copy.start()
        to_blocks.append(copy)

    for s in (1, 2, 0):
        forward_plane(s)

    wait_bytes(blocks.at[pl.ds(0, 3)], come.at[BLOCK])
    pieces[pos] = (((blocks[0] + blocks[1]) + blocks[2]) + blocks[3]).astype(BF16)
    to_pieces = []
    for i, k in enumerate(around):
        copy = copy_to(pieces.at[pos], pieces.at[pos], sent.at[PIECE], come.at[PIECE], along(k))
        copy.start()
        to_pieces.append(copy)
    wait_bytes(pieces.at[pl.ds(0, 7)], come.at[PIECE])

    for q in range(4):
        grad[rows_at(q, 3, 3), q * 128 : (q + 1) * 128] = jnp.concatenate([pieces[2 * q], pieces[2 * q + 1]], axis=0)
    near_grads, far_grads = {}, {}

    def forward_grad(s):
        if s < 3:
            wait_bytes(grad.at[pl.ds(0, 32)], come.at[NEAR_GRAD + s])
        for q in range(4):
            part = grad.at[rows_at(q, 3, s), q * 128 : (q + 1) * 128]
            for e in range(3):
                far_grads[q, e, s] = copy_to(
                    part, part, sent.at[GRAD], come.at[GRAD], chip_of(q, e)
                )
                far_grads[q, e, s].start()

    for q in range(4):
        part = grad.at[rows_at(q, 3, 3), q * 128 : (q + 1) * 128]
        for e in range(3):
            near_grads[q, e] = copy_to(
                part, part, sent.at[NEAR_GRAD + e], come.at[NEAR_GRAD + e], chip_of((q + 2) % 4, e)
            )
            near_grads[q, e].start()
    forward_grad(3)
    for s in (1, 2, 0):
        forward_grad(s)
    wait_bytes(planes.at[pl.ds(0, 3)], come.at[PLANE])
    for r in range(4):

        def lay(slot, carry):
            bit = [rem(div(slot, 1 << ((d - r) % 4)), 2) for d in range(4)]
            quarter = bit[2] * 2 + bit[3]
            for b in range(2):
                for a in range(2):
                    first = pl.multiple_of((a * 8 + 2 * r + b) * 32 + bit[1] * 16, 16)
                    old_full[bit[0], quarter, pl.ds(first, 16), :] = planes[r, slot, b, a]
            return carry

        lax.fori_loop(0, 16, lay, 0)

    wait_bytes(grad.at[pl.ds(0, 384)], come.at[GRAD])

    def eye_of(m):
        row = lax.broadcasted_iota(jnp.int32, (128, 512), 0) + m * 128
        return (row == lax.broadcasted_iota(jnp.int32, (128, 512), 1)).astype(F32)

    def flip(m, carry):
        rows = pl.ds(pl.multiple_of(m * 128, 128), 128)
        grad_t[rows, :] = grad[:, rows].T
        return carry

    lax.fori_loop(0, 4, flip, 0, unroll=True)

    def gram(m, carry):
        rows = pl.ds(pl.multiple_of(m * 128, 128), 128)
        eye = eye_of(m)
        sums_now = []
        for chain in range(2):
            left, right = (grad_t, grad) if chain == 0 else (grad, grad_t)
            term = dot(left[rows, :], right[...])
            quarters = [old_full[chain, q, rows, :] for q in range(4)]
            value = jnp.concatenate(quarters, axis=1) + term
            new_full[chain, rows, :] = value
            damped = value + DAMPING * eye
            sums_now.append(carry[chain] + jnp.sum(damped * damped, axis=0, keepdims=True))
        return tuple(sums_now)

    zero = jnp.zeros((1, 512), F32)
    squares = lax.fori_loop(0, 4, gram, (zero, zero), unroll=True)
    own_first = pl.multiple_of(z_lo * 32 + 16 * core, 16)
    other_first = pl.multiple_of(z_lo * 32 + 16 * other, 16)
    outs, sends = [], []
    for chain in range(2):
        outs.append(
            pltpu.make_async_copy(
                new_full.at[chain, pl.ds(own_first, 16)], stats.at[2 * chain + core], here.at[4]
            )
        )
        sends.append(
            copy_to(
                new_full.at[chain, pl.ds(other_first, 16)], stats.at[2 * chain + core],
                sent.at[OUT], come.at[OUT], partner,
            )
        )
        outs[-1].start()
        sends[-1].start()

    scales = [2.5 / jnp.sqrt(jnp.sum(part, axis=1, keepdims=True)) for part in squares]
    quarters = [jnp.sqrt(jnp.sqrt(scale)) for scale in scales]

    def begin(m, carry):
        rows = pl.ds(pl.multiple_of(m * 128, 128), 128)
        eye = eye_of(m)
        for chain in range(2):
            iterate = scales[chain] * (new_full[chain, rows, :] + DAMPING * eye)
            factor = ((5.0 * eye - iterate) * 0.25).astype(BF16)
            factor0[chain, rows, :] = factor
            factor0[chain, pl.ds(pl.multiple_of(m * 128 + 512, 128), 128), :] = factor
            high = iterate.astype(BF16)
            split[chain, rows, :512] = high
            split[chain, rows, 512:] = (iterate - high.astype(F32)).astype(BF16)
        return carry

    lax.fori_loop(0, 4, begin, 0, unroll=True)

    def multiply(step, carry):
        for chain in range(2):
            iterate = dot(split[chain], factor0[chain])
            high = iterate.astype(BF16)
            split[chain, :, :512] = high
            split[chain, :, 512:] = (iterate - high.astype(F32)).astype(BF16)
        return carry

    lax.fori_loop(0, 3, multiply, 0)

    row_ids = lax.broadcasted_iota(jnp.int32, (256, 512), 0)
    column_ids = lax.broadcasted_iota(jnp.int32, (256, 512), 1)
    for top in range(2):
        rows = slice(256 * top, 256 * top + 256)
        eye = (row_ids + 256 * top == column_ids).astype(F32)
        for chain in range(2):
            iterate = dot(split[chain, rows, :], factor0[chain])
            factor1[chain, rows, :] = ((5.0 * eye - iterate) * 0.25).astype(BF16)

    chip_rows = pl.ds(pl.multiple_of(z_lo * 32, 32), 32)
    right_root = (quarters[1] * dot(factor0[1, chip_rows, :], factor1[1])).astype(BF16)
    for top in range(2):
        rows = slice(256 * top, 256 * top + 256)
        root[rows, :] = (quarters[0] * dot(factor0[0, rows, :], factor1[0])).astype(BF16)
    inner = dot(right_root, grad[...])
    high = inner.astype(BF16)
    rest = inner - high.astype(F32)
    middle = rest.astype(BF16)
    low = (rest - middle.astype(F32)).astype(BF16)
    total = dot(jnp.concatenate([low, middle, high], axis=0), root[...])
    total = (total[:32] + total[32:64]) + total[64:]
    upd[...] = total * math.sqrt(512)
    outs.append(
        pltpu.make_async_copy(
            upd.at[pl.ds(pl.multiple_of(16 * core, 16), 16)], update.at[core], here.at[4]
        )
    )
    sends.append(
        copy_to(
            upd.at[pl.ds(pl.multiple_of(16 * other, 16), 16)], update.at[core],
            sent.at[OUT], come.at[OUT], partner,
        )
    )
    outs[-1].start()
    sends[-1].start()

    wait_bytes(new_full.at[0, pl.ds(0, 48)], here.at[4])
    for sems in (come, sent):
        wait_bytes(new_full.at[0, pl.ds(0, 48)], sems.at[OUT])
    for t in range(2):
        wait_bytes(og_v.at[1], sent.at[SWAP + t])
    wait_bytes(old_v.at[0], sent.at[OLD])
    for s in range(4):
        wait_bytes(got0.at[s], sent.at[SUM + s])
    wait_bytes(got1, sent.at[MID])
    wait_bytes(parts, sent.at[PART])
    wait_bytes(blocks.at[pl.ds(0, 3)], sent.at[BLOCK])
    wait_bytes(pieces.at[pl.ds(0, 7)], sent.at[PIECE])
    for e in range(3):
        wait_bytes(grad.at[pl.ds(0, 32)], sent.at[NEAR_GRAD + e])
        wait_bytes(planes.at[0, pl.ds(0, 4)], sent.at[NEAR_PLANE + e])
    wait_bytes(grad.at[pl.ds(0, 384)], sent.at[GRAD])
    wait_bytes(old_full.at[0, 0, pl.ds(0, 240)], sent.at[COLUMN])
    wait_bytes(planes.at[pl.ds(0, 3)], sent.at[PLANE])


def on_device(activations, out_grads, stats_old):
    dma = pltpu.SemaphoreType.DMA
    vmem = pltpu.VMEM
    anywhere = pl.BlockSpec(memory_space=pl.ANY)
    return pl.pallas_call(
        kernel,
        out_shape=(
            pltpu.VMEM((4, 16, 512), F32),
            pltpu.VMEM((2, 16, 512), F32),
        ),
        in_specs=[anywhere] * 3,
        out_specs=(pl.BlockSpec(memory_space=pltpu.VMEM),) * 2,
        scratch_shapes=[
            vmem((2, 512, 512), BF16),
            vmem((2, 512, 512), BF16),
            vmem((2, 2, 16, 512), F32),
            vmem((4, 512, 128), F32),
            vmem((4, 4, 3, 32, 128), F32),
            vmem((4, 3, 32, 128), F32),
            vmem((8, 16, 128), F32),
            vmem((7, 16, 128), F32),
            vmem((4, 16, 128), F32),
            vmem((8, 16, 128), BF16),
            vmem((512, 512), BF16),
            vmem((512, 512), BF16),
            vmem((8, 2, 16, 128), F32),
            vmem((4, 16, 2, 2, 16, 128), F32),
            vmem((2, 4, 512, 128), F32),
            vmem((2, 512, 512), F32),
            vmem((2, 1024, 512), BF16),
            vmem((2, 512, 512), BF16),
            vmem((2, 512, 1024), BF16),
            vmem((512, 512), BF16),
            vmem((32, 512), F32),
            dma((5,)),
            dma((21,)),
            dma((21,)),
            pltpu.SemaphoreType.REGULAR((4,)),
        ],
        compiler_params=pltpu.CompilerParams(
            collective_id=0, has_side_effects=True, vmem_limit_bytes=56 * 1024 * 1024
        ),
    )(activations, out_grads, stats_old)


def solution(mesh):
    in_specs = (P(("rep", "grp"), None), P(("rep", "grp"), None), P(None, "grp", None))
    out_specs = (P(None, "grp", None), P(None, "grp", None))
    return jax.shard_map(
        on_device, mesh=mesh, in_specs=in_specs, out_specs=out_specs, check_vma=False
    )
```

time: 82 us -> 78.9 us (0.962)
  Pallas kernels: 80 us -> 76.8 us
    pallas_call x1, Pallas kernels: 80 us -> 76.8 us  [on_device(): pl.pallas_call(kernel, out_shape=(pltpu.VMEM((4, 16, 512), F32), pltpu.VM...]
where the time goes in v3:
time: 78.9 us; the launch traced here: 78.8 us
  Pallas kernels  76.8 us (97%)
  local copies, waits for them, and re-layouts  1.29 us (2%)
    pallas_call x1, Pallas kernels, on_device(): pl.pallas_call(kernel, out_shape=(pltpu.VMEM((4, 16, 512), F32), pltpu.VM...  76.8 us

profile of v3, /device:TPU:1, one launch (start us, length us, event | category | flops | bytes accessed | tf_op | source)
XLA Modules:
  0.0 78.8 jit_solution(8516109465771667785)
XLA Ops:
  0.6 76.8 %shard_map.50 = (f32[4,16,512]{2,1,0:T(8,128)S(1)}, f32[2,16,512]{2,1,0:T(8,128)S(1)}) custom-call(bf16[512,512]{1,0:T(8,128)(2,1)} %act.1, bf16[512,1024]{1,0:T(8,128)(2,1)} %og.1, f32[4,16,512]{2,1,0:T(8,128)} %old.1), custom_call_target="tpu_custom_call" | custom-call | tf_op jit(solution)/shard_map/pallas_call | solution.py:445
  77.5 0.7 copy.7
  78.1 0.6 copy.8

commit v4 on v3

--- a/solution.py
+++ b/solution.py
@@ -49,7 +49,7 @@
 def kernel(
     act, og, old, stats, update,
     act_v, og_v, old_v, acc, got0, got1, shard, parts, blocks, pieces, grad, grad_t,
-    column, planes, old_full, new_full, factor0, factor1, split, root, upd,
+    column, planes, old_full, new_full, factor0, factor1, left, square, right, root, upd,
     here, sent, come, know,
 ):
     rep, grp = lax.axis_index("rep"), lax.axis_index("grp")
@@ -59,23 +59,26 @@
     z = z_hi * 16 + z_lo
     blk, pos = div(z, 8), rem(z, 8)
     other = 1 - core
-
-    def device(x_at, y_at, z_at, core_at):
+    tile = rem(core + (x + y + z), 2)
+    other_tile = 1 - tile
+
+    def device(x_at, y_at, z_at, tile_at):
+        core_at = rem(tile_at + (x_at + y_at + z_at), 2)
         return {"rep": (x_at * 4 + y_at) * 2 + div(z_at, 16), "grp": rem(z_at, 16) * 2 + core_at}
 
     def along(k):
-        return device(x, y, rem(z + (k + 32), 32), core)
-
-    partner = device(x, y, z, other)
+        return device(x, y, rem(z + (k + 32), 32), tile)
+
+    partner = device(x, y, z, other_tile)
     x_at = [x + 1 - 2 * rem(x, 2), 3 - x]
     y_at = [y + 1 - 2 * rem(y, 2), 3 - y]
     bits = [rem(rem(x, 2) + div(x, 2), 2), rem(rem(y, 2) + div(y, 2), 2), div(x, 2), div(y, 2)]
-    hops = [device(x_at[0], y, z, core), device(x, y_at[0], z, core), device(x_at[1], y, z, core), device(x, y_at[1], z, core)]
+    hops = [device(x_at[0], y, z, tile), device(x, y_at[0], z, tile), device(x_at[1], y, z, tile), device(x, y_at[1], z, tile)]
     across = [
-        device(x_at[0], y_at[0], z, core),
-        device(x_at[1], y_at[0], z, core),
-        device(x_at[1], y_at[1], z, core),
-        device(x_at[0], y_at[1], z, core),
+        device(x_at[0], y_at[0], z, tile),
+        device(x_at[1], y_at[0], z, tile),
+        device(x_at[1], y_at[1], z, tile),
+        device(x_at[0], y_at[1], z, tile),
     ]
 
     def chip_of(d, e):
@@ -93,13 +96,13 @@
     for near in [partner, *hops, *across, along(1), along(-1)]:
         pl.semaphore_signal(barrier, inc=1, device_id=near, device_id_type=MESH)
 
-    own_cols = pl.ds(pl.multiple_of(core * 512, 512), 512)
-    other_cols = pl.ds(pl.multiple_of(other * 512, 512), 512)
+    own_cols = pl.ds(pl.multiple_of(tile * 512, 512), 512)
+    other_cols = pl.ds(pl.multiple_of(other_tile * 512, 512), 512)
     loads = [
         pltpu.make_async_copy(act, act_v.at[0], here.at[0]),
         pltpu.make_async_copy(og.at[:, own_cols], og_v.at[0], here.at[0]),
-        pltpu.make_async_copy(old.at[core], old_v.at[core, 0], here.at[1]),
-        pltpu.make_async_copy(old.at[core + 2], old_v.at[core, 1], here.at[1]),
+        pltpu.make_async_copy(old.at[tile], old_v.at[core, 0], here.at[1]),
+        pltpu.make_async_copy(old.at[tile + 2], old_v.at[core, 1], here.at[1]),
     ]
     for load in loads:
         load.start()
@@ -120,8 +123,8 @@
         ]
     pair = sent.at[OLD], come.at[OLD], partner
     swaps += [
-        copy_to(old.at[other], old_v.at[core, 0], *pair),
-        copy_to(old.at[other + 2], old_v.at[core, 1], *pair),
+        copy_to(old.at[other_tile], old_v.at[core, 0], *pair),
+        copy_to(old.at[other_tile + 2], old_v.at[core, 1], *pair),
     ]
     for swap in swaps:
         swap.start()
@@ -138,6 +141,8 @@
 
     wait_bytes(og_v, here.at[0])
     local_term(0, 0, 512, False)
+    pl.semaphore_wait(know.at[0], 2)
+    spread(1)
     for t in range(2):
         wait_bytes(og_v.at[1], come.at[SWAP + t])
         local_term(1, 256 * t, 256, True)
@@ -153,8 +158,6 @@
                     acc.at[q, rows_at(q, e, s)], got0.at[s, q, e], sent.at[SUM + s], come.at[SUM + s], chip_of(q, e)
                 )
                 sums[q, e, s].start()
-    pl.semaphore_wait(know.at[0], 2)
-    spread(1)
     wait_bytes(old_v.at[0], here.at[1])
     wait_bytes(old_v.at[0], come.at[OLD])
 
@@ -325,8 +328,8 @@
         eye = eye_of(m)
         sums_now = []
         for chain in range(2):
-            left, right = (grad_t, grad) if chain == 0 else (grad, grad_t)
-            term = dot(left[rows, :], right[...])
+            one, two = (grad_t, grad) if chain == 0 else (grad, grad_t)
+            term = dot(one[rows, :], two[...])
             quarters = [old_full[chain, q, rows, :] for q in range(4)]
             value = jnp.concatenate(quarters, axis=1) + term
             new_full[chain, rows, :] = value
@@ -342,12 +345,12 @@
     for chain in range(2):
         outs.append(
             pltpu.make_async_copy(
-                new_full.at[chain, pl.ds(own_first, 16)], stats.at[2 * chain + core], here.at[4]
+                new_full.at[chain, pl.ds(own_first, 16)], stats.at[2 * chain + tile], here.at[4]
             )
         )
         sends.append(
             copy_to(
-                new_full.at[chain, pl.ds(other_first, 16)], stats.at[2 * chain + core],
+                new_full.at[chain, pl.ds(other_first, 16)], stats.at[2 * chain + tile],
                 sent.at[OUT], come.at[OUT], partner,
             )
         )
@@ -362,25 +365,33 @@
         eye = eye_of(m)
         for chain in range(2):
             iterate = scales[chain] * (new_full[chain, rows, :] + DAMPING * eye)
-            factor = ((5.0 * eye - iterate) * 0.25).astype(BF16)
-            factor0[chain, rows, :] = factor
-            factor0[chain, pl.ds(pl.multiple_of(m * 128 + 512, 128), 128), :] = factor
+            factor0[chain, rows, :] = ((5.0 * eye - iterate) * 0.25).astype(BF16)
             high = iterate.astype(BF16)
-            split[chain, rows, :512] = high
-            split[chain, rows, 512:] = (iterate - high.astype(F32)).astype(BF16)
+            left[chain, rows, :512] = high
+            left[chain, rows, 512:] = (iterate - high.astype(F32)).astype(BF16)
         return carry
 
     lax.fori_loop(0, 4, begin, 0, unroll=True)
 
-    def multiply(step, carry):
-        for chain in range(2):
-            iterate = dot(split[chain], factor0[chain])
-            high = iterate.astype(BF16)
-            split[chain, :, :512] = high
-            split[chain, :, 512:] = (iterate - high.astype(F32)).astype(BF16)
-        return carry
-
-    lax.fori_loop(0, 3, multiply, 0)
+    def pieces_of(value):
+        high = value.astype(BF16)
+        return high, (value - high.astype(F32)).astype(BF16)
+
+    def product(a, a_high, chain):
+        return dot(a, right[chain, :1024, :]) + dot(a_high, right[chain, 1024:, :])
+
+    def keep_right(chain, high, low):
+        right[chain, :512, :] = high
+        right[chain, 512:1024, :] = high
+        right[chain, 1024:, :] = low
+
+    for chain in range(2):
+        high, low = pieces_of(dot(factor0[chain], factor0[chain]))
+        square[chain, :, :512] = high
+        square[chain, :, 512:] = low
+        keep_right(chain, high, low)
+    for chain in range(2):
+        keep_right(chain, *pieces_of(product(square[chain], square[chain, :, :512], chain)))
 
     row_ids = lax.broadcasted_iota(jnp.int32, (256, 512), 0)
     column_ids = lax.broadcasted_iota(jnp.int32, (256, 512), 1)
@@ -388,7 +399,7 @@
         rows = slice(256 * top, 256 * top + 256)
         eye = (row_ids + 256 * top == column_ids).astype(F32)
         for chain in range(2):
-            iterate = dot(split[chain, rows, :], factor0[chain])
+            iterate = product(left[chain, rows, :], left[chain, rows, :512], chain)
             factor1[chain, rows, :] = ((5.0 * eye - iterate) * 0.25).astype(BF16)
 
     chip_rows = pl.ds(pl.multiple_of(z_lo * 32, 32), 32)
@@ -406,12 +417,12 @@
     upd[...] = total * math.sqrt(512)
     outs.append(
         pltpu.make_async_copy(
-            upd.at[pl.ds(pl.multiple_of(16 * core, 16), 16)], update.at[core], here.at[4]
+            upd.at[pl.ds(pl.multiple_of(16 * core, 16), 16)], update.at[tile], here.at[4]
         )
     )
     sends.append(
         copy_to(
-            upd.at[pl.ds(pl.multiple_of(16 * other, 16), 16)], update.at[core],
+            upd.at[pl.ds(pl.multiple_of(16 * other, 16), 16)], update.at[tile],
             sent.at[OUT], come.at[OUT], partner,
         )
     )
@@ -438,11 +449,22 @@
     wait_bytes(planes.at[pl.ds(0, 3)], sent.at[PLANE])
 
 
+def write(stats, update, stats_out, update_out, sem):
+    copies = [
+        pltpu.make_async_copy(stats, stats_out, sem.at[0]),
+        pltpu.make_async_copy(update, update_out, sem.at[1]),
+    ]
+    for copy in copies:
+        copy.start()
+    for copy in copies:
+        copy.wait()
+
+
 def on_device(activations, out_grads, stats_old):
     dma = pltpu.SemaphoreType.DMA
     vmem = pltpu.VMEM
     anywhere = pl.BlockSpec(memory_space=pl.ANY)
-    return pl.pallas_call(
+    results = pl.pallas_call(
         kernel,
         out_shape=(
             pltpu.VMEM((4, 16, 512), F32),
@@ -467,9 +489,11 @@
             vmem((4, 16, 2, 2, 16, 128), F32),
             vmem((2, 4, 512, 128), F32),
             vmem((2, 512, 512), F32),
-            vmem((2, 1024, 512), BF16),
+            vmem((2, 512, 512), BF16),
             vmem((2, 512, 512), BF16),
             vmem((2, 512, 1024), BF16),
+            vmem((2, 512, 1024), BF16),
+            vmem((2, 1536, 512), BF16),
             vmem((512, 512), BF16),
             vmem((32, 512), F32),
             dma((5,)),
@@ -481,6 +505,16 @@
             collective_id=0, has_side_effects=True, vmem_limit_bytes=56 * 1024 * 1024
         ),
     )(activations, out_grads, stats_old)
+    return pl.pallas_call(
+        write,
+        out_shape=(
+            jax.ShapeDtypeStruct((4, 16, 512), F32),
+            jax.ShapeDtypeStruct((2, 16, 512), F32),
+        ),
+        in_specs=[anywhere] * 2,
+        out_specs=(anywhere, anywhere),
+        scratch_shapes=[dma((2,))],
+    )(*[pltpu.with_memory_space_constraint(result, pltpu.VMEM) for result in results])
 
 
 def solution(mesh):

time: 78.9 us -> 76.2 us (0.966)
  Pallas kernels: 76.8 us -> 75.5 us
  local copies, waits for them, and re-layouts: 1.29 us -> 0 us
    pallas_call x1, Pallas kernels: 76.8 us -> 74.8 us  [on_device(): pl.pallas_call(kernel, out_shape=(pltpu.VMEM((4, 16, 512), F32), pltpu.VM...]
    unnamed x2 -> x0, local copies, waits for them, and re-layouts: 1.29 us -> none
where the time goes in v4:
time: 76.2 us; the launch traced here: 76.1 us
  Pallas kernels  75.5 us (99%)
    pallas_call x1, Pallas kernels, on_device(): pl.pallas_call(kernel, out_shape=(pltpu.VMEM((4, 16, 512), F32), pltpu.VM...  74.8 us

profile of v4, /device:TPU:1, one launch (start us, length us, event | category | flops | bytes accessed | tf_op | source)
XLA Modules:
  0.0 76.1 jit_solution(10495657444085003234)
XLA Ops:
  0.6 74.8 %shard_map.50 = (f32[4,16,512]{2,1,0:T(8,128)S(1)}, f32[2,16,512]{2,1,0:T(8,128)S(1)}) custom-call(bf16[512,512]{1,0:T(8,128)(2,1)} %act.1, bf16[512,1024]{1,0:T(8,128)(2,1)} %og.1, f32[4,16,512]{2,1,0:T(8,128)} %old.1), custom_call_target="tpu_custom_call" | custom-call | tf_op jit(solution)/shard_map/pallas_call | solution.py:467
  75.4 0.7 shard_map.51

commit v5 on v4

--- a/solution.py
+++ b/solution.py
@@ -15,8 +15,8 @@
 ITERS = 2
 
 
-SWAP, OLD, SUM, MID, PART, BLOCK, PIECE, NEAR_GRAD, GRAD, COLUMN, NEAR_PLANE, PLANE, OUT = (
-    0, 2, 3, 7, 8, 9, 10, 11, 14, 15, 16, 19, 20
+SWAP, OLD, SUM, MID, PART, BLOCK, NEAR_GRAD, GRAD, COLUMN, NEAR_PLANE, PLANE, OUT = (
+    0, 2, 3, 7, 8, 9, 10, 14, 15, 16, 19, 20
 )
 
 
@@ -83,6 +83,11 @@
 
     def chip_of(d, e):
         return (across[d], hops[d], hops[(d + 1) % 4])[e]
+
+    def place_of(d, e):
+        flip_x, flip_y = (e in (0, 1), e in (0, 2)) if d % 2 == 0 else (e in (0, 2), e in (0, 1))
+        along_x, along_y = (d // 2, d // 2) if d % 2 == 0 else ((d + 1) % 4 // 2, d // 2)
+        return (x_at[along_x] if flip_x else x), (y_at[along_y] if flip_y else y)
 
     def number_of(d, e):
         first, second = bits[d], bits[(d + 1) % 4]
@@ -263,21 +268,35 @@
         forward_plane(s)
 
     wait_bytes(blocks.at[pl.ds(0, 3)], come.at[BLOCK])
-    pieces[pos] = (((blocks[0] + blocks[1]) + blocks[2]) + blocks[3]).astype(BF16)
-    to_pieces = []
-    for i, k in enumerate(around):
-        copy = copy_to(pieces.at[pos], pieces.at[pos], sent.at[PIECE], come.at[PIECE], along(k))
-        copy.start()
-        to_pieces.append(copy)
-    wait_bytes(pieces.at[pl.ds(0, 7)], come.at[PIECE])
-
-    for q in range(4):
-        grad[rows_at(q, 3, 3), q * 128 : (q + 1) * 128] = jnp.concatenate([pieces[2 * q], pieces[2 * q + 1]], axis=0)
-    near_grads, far_grads = {}, {}
+    pieces[...] = (((blocks[0] + blocks[1]) + blocks[2]) + blocks[3]).astype(BF16)
+    quarter_at = div(pos, 2)
+
+    n = quarter_at
+    picks = [
+        div((1 - n) * (2 - n) * (3 - n), 6), div(n * (2 - n) * (3 - n), 2), div(n * (n - 1) * (3 - n), 2), div(n * (n - 1) * (n - 2), 6)
+    ]
+
+    def choose(values):
+        return sum(pick * value for pick, value in zip(picks, values))
+
+    piece_first = choose([128 * number_of(q, 3) + 32 * number_of((q + 2) % 4, 3) for q in range(4)]) + 16 * rem(pos, 2)
+    piece_at = grad.at[
+        pl.ds(pl.multiple_of(piece_first, 16), 16), pl.ds(pl.multiple_of(quarter_at * 128, 128), 128)
+    ]
+    for e in (0, 3, 1, 2):
+        for k in (-4, 3, -3, 2, -2, 1, -1, 0):
+            if e == 3 and k == 0:
+                continue
+            z_to = rem(z + (k + 32), 32)
+            to_x = choose([place_of((q + 2) % 4, e)[0] for q in range(4)])
+            to_y = choose([place_of((q + 2) % 4, e)[1] for q in range(4)])
+            copy_to(pieces, piece_at, sent.at[NEAR_GRAD + e], come.at[NEAR_GRAD + e], device(to_x, to_y, z_to, tile)).start()
+    keep_piece = pltpu.make_async_copy(pieces, piece_at, here.at[2])
+    keep_piece.start()
+    far_grads = {}
 
     def forward_grad(s):
-        if s < 3:
-            wait_bytes(grad.at[pl.ds(0, 32)], come.at[NEAR_GRAD + s])
+        wait_bytes(old_full.at[0, 0, pl.ds(0, 56 if s == 3 else 64)], come.at[NEAR_GRAD + s])
         for q in range(4):
             part = grad.at[rows_at(q, 3, s), q * 128 : (q + 1) * 128]
             for e in range(3):
@@ -286,15 +305,8 @@
                 )
                 far_grads[q, e, s].start()
 
-    for q in range(4):
-        part = grad.at[rows_at(q, 3, 3), q * 128 : (q + 1) * 128]
-        for e in range(3):
-            near_grads[q, e] = copy_to(
-                part, part, sent.at[NEAR_GRAD + e], come.at[NEAR_GRAD + e], chip_of((q + 2) % 4, e)
-            )
-            near_grads[q, e].start()
-    forward_grad(3)
-    for s in (1, 2, 0):
+    keep_piece.wait()
+    for s in (3, 1, 2, 0):
         forward_grad(s)
     wait_bytes(planes.at[pl.ds(0, 3)], come.at[PLANE])
     for r in range(4):
@@ -440,7 +452,7 @@
     wait_bytes(got1, sent.at[MID])
     wait_bytes(parts, sent.at[PART])
     wait_bytes(blocks.at[pl.ds(0, 3)], sent.at[BLOCK])
-    wait_bytes(pieces.at[pl.ds(0, 7)], sent.at[PIECE])
+    wait_bytes(old_full.at[0, 0, pl.ds(0, 56)], sent.at[NEAR_GRAD + 3])
     for e in range(3):
         wait_bytes(grad.at[pl.ds(0, 32)], sent.at[NEAR_GRAD + e])
         wait_bytes(planes.at[0, pl.ds(0, 4)], sent.at[NEAR_PLANE + e])
@@ -482,7 +494,7 @@
             vmem((8, 16, 128), F32),
             vmem((7, 16, 128), F32),
             vmem((4, 16, 128), F32),
-            vmem((8, 16, 128), BF16),
+            vmem((16, 128), BF16),
             vmem((512, 512), BF16),
             vmem((512, 512), BF16),
             vmem((8, 2, 16, 128), F32),

time: 76.2 us -> 74.2 us (0.974)
  Pallas kernels: 75.5 us -> 73.4 us
    pallas_call x1, Pallas kernels: 74.8 us -> 72.7 us  [on_device(): pl.pallas_call(kernel, out_shape=(pltpu.VMEM((4, 16, 512), F32), pltpu.VM...]
where the time goes in v5:
time: 74.2 us; the launch traced here: 74.1 us
  Pallas kernels  73.4 us (99%)
    pallas_call x1, Pallas kernels, on_device(): pl.pallas_call(kernel, out_shape=(pltpu.VMEM((4, 16, 512), F32), pltpu.VM...  72.7 us

profile of v5, /device:TPU:1, one launch (start us, length us, event | category | flops | bytes accessed | tf_op | source)
XLA Modules:
  0.0 74.1 jit_solution(13916321327704112788)
XLA Ops:
  0.6 72.7 %shard_map.50 = (f32[4,16,512]{2,1,0:T(8,128)S(1)}, f32[2,16,512]{2,1,0:T(8,128)S(1)}) custom-call(bf16[512,512]{1,0:T(8,128)(2,1)} %act.1, bf16[512,1024]{1,0:T(8,128)(2,1)} %og.1, f32[4,16,512]{2,1,0:T(8,128)} %old.1), custom_call_target="tpu_custom_call" | custom-call | tf_op jit(solution)/shard_map/pallas_call | solution.py:479
  73.4 0.7 shard_map.51
